TPU v7x, 256 devices: a whole 4x4x8 slice. The times are simulated.
256 devices in a mesh: gx: 8 (over x, core), gy: 32 (over y, z).
Axes of the slice: x: 4, y: 4, z: 8, core: 2. Of those that a mesh axis runs over, the one named last changes fastest.
Arguments:
- features: float32 [64, 524288], P(None, ('gx', 'gy')), may hold values from -6 to 6
- cotangent: float32 [64, 524288], P(None, ('gx', 'gy')), may hold values from -6 to 6
- edge_src: int32 [8, 524288], P(None, ('gx', 'gy')), may hold values from 0 to 2559
- send_rows: int32 [4, 32768], P(None, ('gx', 'gy')), may hold values from 0 to 2047
- fine_to_coarse: int32 [524288], P(('gx', 'gy')), may hold values from 0 to 2047
- coarse_to_fine: int32 [524288], P(('gx', 'gy')), may hold values from 0 to 2047
- coarse_edges: int32 [2, 8192], replicated, may hold values from 0 to 2047
- edge_in: float32 [64, 128], replicated, may hold values from -0.5 to 0.5
- edge_out: float32 [64, 64], replicated, may hold values from -0.75 to 0.75
- node_in: float32 [64, 128], replicated, may hold values from -0.5 to 0.5
- node_out: float32 [64, 64], replicated, may hold values from -0.75 to 0.75
- coarse_in: float32 [64, 64], replicated, may hold values from -0.75 to 0.75
- coarse_out: float32 [64, 64], replicated, may hold values from -0.75 to 0.75
- coarse_mix: float32 [64, 64], replicated, may hold values from -0.75 to 0.75
- up_in: float32 [64, 128], replicated, may hold values from -0.5 to 0.5
- up_out: float32 [64, 64], replicated, may hold values from -0.75 to 0.75
- biases: float32 [4, 64], replicated, may hold values from -3 to 3
Outputs:
- output: float32 [64, 524288], P(None, ('gx', 'gy'))
- grad_features: float32 [64, 524288], P(None, ('gx', 'gy'))
- grad_edge_in: float32 [64, 128], replicated
- grad_edge_out: float32 [64, 64], replicated
- grad_node_in: float32 [64, 128], replicated
- grad_node_out: float32 [64, 64], replicated
- grad_coarse_in: float32 [64, 64], replicated
- grad_coarse_out: float32 [64, 64], replicated
- grad_coarse_mix: float32 [64, 64], replicated
- grad_up_in: float32 [64, 128], replicated
- grad_up_out: float32 [64, 64], replicated
- grad_biases: float32 [4, 64], replicated
Inputs may be any that keep to these rules, and one draw needn't show every extreme that they name: `edge_src`: indexes the receiver partition's 2048 own nodes, then the four received packets in the order of the first step. `send_rows`: partition-local node numbers.
All inputs are finite; a program needn't handle non-finite values.
Results may differ from a plain program's by a relative error of at most 0.0003.
Values sent between devices are 32-bit elements; how exact they have to be, the bound alone decides.
A program may use at most 64 MiB of HBM per device.

v0:
```python
from functools import partial
import math
import jax
import jax.numpy as jnp
from jax import lax
from jax.sharding import PartitionSpec as P

COARSE = 2048


def passed_along(value, axis, steps):
    count = lax.axis_size(axis)
    leading, last = (max(0, -steps), min(count, count - steps))
    return lax.ppermute(value, axis, [(source, source + steps) for source in range(leading, last)])


def matmul(left_side, right_side):
    return jnp.dot(
        left_side, right_side, precision=lax.Precision.HIGHEST, preferred_element_type=jnp.float32
    )


def swish(values):
    return values * jax.nn.sigmoid(values)


def fine_update(
    latent, extended, edge_in, edge_out, node_in, node_out, edge_bias, node_bias, sources
):
    feature_count = latent.shape[0]
    receiver_part = matmul(edge_in[:, :feature_count], latent)
    sender_part = matmul(edge_in[:, feature_count:], extended)
    hidden = swish(receiver_part[:, None, :] + sender_part[:, sources] + edge_bias[:, None, None])
    summed = matmul(edge_out, jnp.sum(hidden, axis=1))
    activation = swish(
        matmul(node_in[:, :feature_count], latent)
        + matmul(node_in[:, feature_count:], summed)
        + node_bias[:, None]
    )
    return latent + matmul(node_out, activation)


def coarse_node(pooled, coarse_in, coarse_out, coarse_bias):
    return pooled + matmul(coarse_out, swish(matmul(coarse_in, pooled) + coarse_bias[:, None]))


def coarse_edge(nodes, coarse_mix, coarse_edges):
    gathered = nodes[:, coarse_edges[0]]
    summed = jnp.zeros_like(nodes).at[:, coarse_edges[1]].add(gathered)
    factor = (nodes.shape[1] / coarse_edges.shape[1]) ** 0.5
    return nodes + matmul(coarse_mix, summed) * factor


def up_update(middle, looked, up_in, up_out, up_bias):
    feature_count = middle.shape[0]
    activation = swish(
        matmul(up_in[:, :feature_count], middle)
        + matmul(up_in[:, feature_count:], looked)
        + up_bias[:, None]
    )
    return middle + matmul(up_out, activation)


def block_width(node_count):
    return math.gcd(node_count, 1024)


def one_hot_block(index_block, table_width):
    return (index_block[:, None] == jnp.arange(table_width, dtype=jnp.int32)[None, :]).astype(
        jnp.float32
    )


def pool_nodes(values, index, table_width):
    feature_count, node_count = values.shape
    width = block_width(node_count)
    blocks = node_count // width
    value_blocks = values.reshape(feature_count, blocks, width).transpose(1, 0, 2)
    index_blocks = index.reshape(blocks, width)

    def add_block(total, items):
        return (total + matmul(items[0], one_hot_block(items[1], table_width)), None)

    start = jnp.zeros((feature_count, table_width), jnp.float32)
    total, unused = lax.scan(add_block, start, (value_blocks, index_blocks))
    return total


def look_nodes(table, index):
    feature_count, table_width = table.shape
    node_count = index.shape[0]
    width = block_width(node_count)
    blocks = node_count // width
    index_blocks = index.reshape(blocks, width)

    def read_block(index_block):
        selector = one_hot_block(index_block, table_width)
        return lax.dot_general(
            table,
            selector,
            (((1,), (1,)), ((), ())),
            precision=lax.Precision.HIGHEST,
            preferred_element_type=jnp.float32,
        )

    result = lax.map(read_block, index_blocks)
    return result.transpose(1, 0, 2).reshape(feature_count, node_count)


def pass_rows(packet, offset):
    return passed_along(packet, "gx", offset)


def pass_cols(packet, offset):
    return passed_along(packet, "gy", offset)


def coarse_total(table):
    return lax.psum(table, ("gx", "gy"))


def local(
    features,
    cotangent,
    edge_src,
    send_rows,
    fine_to_coarse,
    coarse_to_fine,
    coarse_edges,
    edge_in,
    edge_out,
    node_in,
    node_out,
    coarse_in,
    coarse_out,
    coarse_mix,
    up_in,
    up_out,
    biases,
):
    local_nodes = features.shape[1]
    halo_rows = send_rows.shape[1]
    pool_scale = (COARSE / (local_nodes * lax.axis_size("gx") * lax.axis_size("gy"))) ** 0.5
    packets = features[:, send_rows]
    extended = jnp.concatenate(
        [
            features,
            pass_rows(packets[:, 0], 1),
            pass_rows(packets[:, 1], -1),
            pass_cols(packets[:, 2], 1),
            pass_cols(packets[:, 3], -1),
        ],
        axis=1,
    )
    middle, fine_back = jax.vjp(
        partial(fine_update, sources=edge_src),
        features,
        extended,
        edge_in,
        edge_out,
        node_in,
        node_out,
        biases[0],
        biases[1],
    )
    pooled_part = pool_nodes(middle, fine_to_coarse, COARSE) * pool_scale
    pooled = coarse_total(pooled_part)
    nodes, node_back = jax.vjp(coarse_node, pooled, coarse_in, coarse_out, biases[2])
    mixed, mix_back = jax.vjp(partial(coarse_edge, coarse_edges=coarse_edges), nodes, coarse_mix)
    looked = look_nodes(mixed, coarse_to_fine)
    output, up_back = jax.vjp(up_update, middle, looked, up_in, up_out, biases[3])
    grad_middle, grad_looked, grad_up_in, grad_up_out, grad_up_bias = up_back(cotangent)
    grad_mixed_part = pool_nodes(grad_looked, coarse_to_fine, COARSE)
    grad_nodes_part, grad_mix = mix_back(grad_mixed_part)
    grad_nodes = coarse_total(grad_nodes_part)
    grad_pooled, grad_coarse_in, grad_coarse_out, grad_coarse_bias = node_back(grad_nodes)
    grad_middle = grad_middle + look_nodes(grad_pooled, fine_to_coarse) * pool_scale
    (
        grad_own,
        grad_ext,
        grad_edge_in,
        grad_edge_out,
        grad_node_in,
        grad_node_out,
        grad_edge_bias,
        grad_node_bias,
    ) = fine_back(grad_middle)
    pieces = [
        grad_ext[:, local_nodes + slot * halo_rows : local_nodes + (slot + 1) * halo_rows]
        for slot in range(4)
    ]
    returned = jnp.stack(
        [
            pass_rows(pieces[0], -1),
            pass_rows(pieces[1], 1),
            pass_cols(pieces[2], -1),
            pass_cols(pieces[3], 1),
        ],
        axis=1,
    )
    grad_features = (
        grad_own
        + grad_ext[:, :local_nodes]
        + jnp.zeros_like(features).at[:, send_rows].add(returned)
    )
    fine_biases = jnp.stack([grad_edge_bias, grad_node_bias, grad_up_bias])
    summed = lax.psum(
        (
            grad_edge_in,
            grad_edge_out,
            grad_node_in,
            grad_node_out,
            grad_mix,
            grad_up_in,
            grad_up_out,
            fine_biases,
        ),
        ("gx", "gy"),
    )
    grad_biases = jnp.stack([summed[7][0], summed[7][1], grad_coarse_bias, summed[7][2]])
    return (
        output,
        grad_features,
        summed[0],
        summed[1],
        summed[2],
        summed[3],
        grad_coarse_in,
        grad_coarse_out,
        summed[4],
        summed[5],
        summed[6],
        grad_biases,
    )


def solution(mesh):
    in_specs = (
        P(None, ("gx", "gy")),
        P(None, ("gx", "gy")),
        P(None, ("gx", "gy")),
        P(None, ("gx", "gy")),
        P(("gx", "gy")),
        P(("gx", "gy")),
        P(),
        P(),
        P(),
        P(),
        P(),
        P(),
        P(),
        P(),
        P(),
        P(),
        P(),
    )
    out_specs = (
        P(None, ("gx", "gy")),
        P(None, ("gx", "gy")),
        P(),
        P(),
        P(),
        P(),
        P(),
        P(),
        P(),
        P(),
        P(),
        P(),
    )
    return jax.shard_map(local, mesh=mesh, in_specs=in_specs, out_specs=out_specs, check_vma=False)
```

profile of v0, /device:TPU:4, one launch (start us, length us, event | category | flops | bytes accessed | tf_op | source)
XLA Modules:
  0.0 1284.9 jit_solution(6008554091809120378)
XLA Ops:
  11.8 4.5 collective-permute-start.2
  16.3 1.9 collective-permute-start.1
  18.3 2.4 collective-permute-start
  24.3 2.9 fusion.81
  27.2 2.9 fusion.102
  35.8 54.7 %gather_fusion.1 = f32[16384,64]{1,0:T(8,128)} fusion(f32[64,2560]{0,1:T(8,128)S(1)} %copy.65, s32[16384]{0:T(1024)S(1)} %broadcast_clamp_fusion), kind=kCustom, calls=%fused_computation.1 | custom fusion | bytes 8454144 | tf_op jit(solution)/shard_map/jvp()/gather | solution.py:33
  90.6 4.8 multiply_reduce_fusion
  100.4 7.0 while.44
  100.5 3.5 fusion.178
  104.0 3.5 fusion.178
  110.1 254.7 %all-reduce.11.cloned.1.call-done = f32[64,2048]{1,0:T(8,128)} async-done(((f32[64,2048]{1,0:T(8,128)}), f32[64,2048]{1,0:T(8,128)}) %all-reduce.11.cloned.1.call-update) | async-done | bytes 524304 | tf_op jit(solution)/shard_map/psum | solution.py:119
  370.4 90.5 %scatter_custom_fusion = f32[64,2048]{0,1:T(8,128)S(1)} fusion(s32[8192]{0:T(1024)} %bitcast.245, f32[64,2048]{0,1:T(8,128)} %copy.67, s32[8192]{0:T(1024)} %broadcast_clamp_fusion.2, f32[]{:T(128)} %constant.19.clone.1), kind=kCustom, calls=%fused_computation.44 | custom fusion | flops 524288 | bytes 524800 | tf_op jit(solution)/shard_map/jvp()/scatter-add | solution.py:49
  460.9 2.1 fusion.29
  463.0 11.0 while.42
  463.1 5.5 fusion.174
  468.6 5.5 fusion.174
  474.1 2.2 fusion.96
  476.3 2.3 convolution_bitcast_fusion.14
  478.6 2.6 fusion.37
  485.0 10.4 while.45
  485.0 5.1 fusion.180
  490.1 5.3 fusion.180
  495.4 2.5 convolution_bitcast_fusion.7
  497.9 2.4 copy.71
  500.2 2.4 copy.70
  502.6 103.6 %scatter_custom_fusion.1 = f32[64,2048]{0,1:T(8,128)} fusion(f32[64,2048]{0,1:T(8,128)} %copy.71, s32[8192]{0:T(1024)} %bitcast.243, f32[]{:T(128)} %constant.19.clone.1, pred[8192]{0:T(1024)(128)(4,1)S(1)} %compare_and_fusion, f32[64,2048]{0,1:T(8,128)} %copy.70, s32[8192]{0:T(1024)S(1)} %broadcast_clamp_fusion.1), kind=kCustom, calls=%fused_computation.42 | custom fusion | flops 1048576 | bytes 1614336 | tf_op jit(solution)/shard_map/transpose(jvp())/scatter-add | solution.py:48
  606.2 2.3 copy.72
  608.6 2.4 fusion.55
  611.0 248.5 %all-reduce.13.cloned.1.call-done = f32[64,2048]{1,0:T(8,128)} async-done(((f32[64,2048]{1,0:T(8,128)}), f32[64,2048]{1,0:T(8,128)}) %all-reduce.13.cloned.1.call-update) | async-done | bytes 524304 | tf_op jit(solution)/shard_map/psum | solution.py:119
  859.5 2.6 fusion.100
  864.6 8.9 while.43
  864.6 4.4 fusion.176
  869.1 4.4 fusion.176
  877.3 2.6 fusion.62
  889.0 5.7 fusion.21
  894.7 3.2 copy-done.1
  898.0 2.5 fusion.95
  900.4 2.5 fusion.104
  902.9 2.1 convolution_bitcast_fusion.13
  905.0 88.0 %scatter_custom_fusion.2 = f32[64,2560]{0,1:T(8,128)S(1)} fusion(s32[16384]{0:T(1024)S(1)} %bitcast.240, f32[16384,64]{1,0:T(8,128)} %bitcast.227, f32[]{:T(128)} %constant.19.clone.1), kind=kCustom, calls=%fused_computation.85 | custom fusion | flops 1048576 | bytes 655872 | tf_op jit(solution)/shard_map/transpose(jvp())/scatter-add | solution.py:33
  993.0 2.2 fusion.103
  998.7 1.9 collective-permute-start.4
  1000.6 1.9 collective-permute-start.7
  1003.8 2.2 collective-permute-start.5
  1009.6 2.5 fusion.65
  1012.1 2.4 fusion.108
  1015.1 3.7 scatter_fusion
  1019.9 246.4 %all-reduce.15.cloned.1.call-done = (f32[64,128]{1,0:T(8,128)}, f32[64,64]{1,0:T(8,128)}, f32[64,128]{1,0:T(8,128)}, f32[64,64]{1,0:T(8,128)}, f32[64,64]{1,0:T(...) async-done(((f32[64,128]{1,0:T(8,128)}, f32[64,64]{1,0:T(8,128)}, f32[64,128]{1,0:T(8,128)}, f32[64,64]{1,0:T(8,128)}, f32[64,64]{1,0:T(8,128)}, ...) | async-done | bytes 164624 | tf_op jit(solution)/shard_map/psum | solution.py:207
  (159 shorter events, 67.9 us)
Async XLA Ops:
  7.2 360.1 %copy-start = (f32[64,64]{1,0:T(8,128)S(1)}, f32[64,64]{1,0:T(8,128)}, u32[]{:S(2)}) copy-start(f32[64,64]{1,0:T(8,128)} %param.37) | copy-start | bytes 49156
  7.2 357.6 %all-reduce.11.cloned.1.call-start = ((), (), s32[]{:S(2)}) async-start(), calls=%async_computation | async-start | bytes 1048576 | tf_op jit(solution)/shard_map/psum | solution.py:119
  10.5 22.6 %collective-permute-start.3 = (f32[64,128]{1,0:T(8,128)S(1)}, f32[64,128]{1,0:T(8,128)S(1)}, u32[]{:S(2)}, u32[]{:S(2)}) collective-permute-start(f32[64,128]{1,0:T(8,128)S(1)} %get-tuple-element.218), channel_id=1, source_target_pairs={{1,0},{2,1},{3,2},{4,3},{5,4},{6,5},{7,6},{8,7},{9,8},{10,9},{11,1... | collective-permute-start | bytes 98312 | tf_op jit(solution)/shard_map/ppermute | solution.py:14
  11.8 21.3 %collective-permute-start.2 = (f32[64,128]{1,0:T(8,128)S(1)}, f32[64,128]{1,0:T(8,128)S(1)}, u32[]{:S(2)}, u32[]{:S(2)}) collective-permute-start(f32[64,128]{1,0:T(8,128)S(1)} %get-tuple-element.219), channel_id=1, source_target_pairs={{0,1},{1,2},{2,3},{3,4},{4,5},{5,6},{6,7},{7,8},{8,9},{9,10},{10,1... | collective-permute-start | bytes 98312 | tf_op jit(solution)/shard_map/ppermute | solution.py:14
  16.3 16.7 %collective-permute-start.1 = (f32[64,128]{1,0:T(8,128)S(1)}, f32[64,128]{1,0:T(8,128)S(1)}, u32[]{:S(2)}, u32[]{:S(2)}) collective-permute-start(f32[64,128]{1,0:T(8,128)S(1)} %get-tuple-element.220), channel_id=1, source_target_pairs={{32,0},{64,32},{96,64},{128,96},{160,128},{192,160},{224,192},{33,... | collective-permute-start | bytes 98312 | tf_op jit(solution)/shard_map/ppermute | solution.py:14
  18.3 14.7 %collective-permute-start = (f32[64,128]{1,0:T(8,128)S(1)}, f32[64,128]{1,0:T(8,128)S(1)}, u32[]{:S(2)}, u32[]{:S(2)}) collective-permute-start(f32[64,128]{1,0:T(8,128)S(1)} %get-tuple-element.221), channel_id=1, source_target_pairs={{0,32},{32,64},{64,96},{96,128},{128,160},{160,192},{192,224},{1,3... | collective-permute-start | bytes 98312 | tf_op jit(solution)/shard_map/ppermute | solution.py:14
  23.7 6.4 copy-start.24
  23.7 12.2 copy-start.23
  27.2 63.4 %copy-start.3 = (f32[64,2048]{0,1:T(8,128)}, f32[64,2048]{0,1:T(8,128)S(1)}, u32[]{:S(2)}) copy-start(f32[64,2048]{0,1:T(8,128)S(1)} %fusion.81) | copy-start | bytes 1572868
  33.1 0.9 copy-start.5
  90.6 4.9 copy-start.22
  90.6 7.0 copy-start.18
  90.6 7.6 copy-start.2
  90.6 9.0 copy-start.29
  90.6 9.8 copy-start.16
  96.8 0.8 copy-start.7
  98.8 0.8 copy-start.15
  100.3 8.3 copy-start.9
  100.4 8.2 copy-start.26
  100.4 8.3 copy-start.19
  100.4 264.3 %copy-start.21 = (f32[64,64]{1,0:T(8,128)S(1)}, f32[64,64]{1,0:T(8,128)}, u32[]{:S(2)}) copy-start(f32[64,64]{1,0:T(8,128)} %param.36) | copy-start | bytes 49156
  107.4 353.4 %copy-start.20 = (f32[64,64]{1,0:T(8,128)S(1)}, f32[64,64]{1,0:T(8,128)}, u32[]{:S(2)}) copy-start(f32[64,64]{1,0:T(8,128)} %param.38) | copy-start | bytes 49156
  108.3 751.2 %all-reduce.13.cloned.1.call-start = ((), (), s32[]{:S(2)}) async-start(), calls=%async_computation.1 | async-start | bytes 1048576 | tf_op jit(solution)/shard_map/psum | solution.py:119
  366.4 0.8 copy-start.17
  463.0 11.1 copy-start.28
  463.0 15.5 %copy-start.25 = (f32[64,64]{1,0:T(8,128)S(1)}, f32[64,64]{1,0:T(8,128)}, u32[]{:S(2)}) copy-start(f32[64,64]{1,0:T(8,128)} %param.40) | copy-start | bytes 49156
  474.0 8.3 copy-start.10
  608.5 657.8 %all-reduce.15.cloned.1.call-start = ((), (), s32[]{:S(2)}) async-start(), calls=%async_computation.2 | async-start | bytes 462848 | tf_op jit(solution)/shard_map/psum | solution.py:207
  862.1 0.8 copy-start.11
  864.6 15.3 %copy-start.30 = (f32[64,64]{1,0:T(8,128)S(1)}, f32[64,64]{1,0:T(8,128)}, u32[]{:S(2)}) copy-start(f32[64,64]{1,0:T(8,128)} %param.35) | copy-start | bytes 49156
  873.5 0.8 copy-start.12
  874.3 7.4 copy-start.8
  874.3 14.6 %copy-start.4 = (f32[64,2048]{0,1:T(8,128)S(1)}, f32[64,2048]{0,1:T(8,128)}, u32[]{:S(2)}) copy-start(f32[64,2048]{0,1:T(8,128)} %copy-done.3) | copy-start | bytes 1572868
  877.3 5.7 copy-start.13
  894.7 3.2 copy-start.1
  897.9 4.9 copy-start.14
  897.9 95.0 %copy-start.6 = (f32[64,2560]{1,0:T(8,128)S(1)}, f32[64,2560]{1,0:T(8,128)}, u32[]{:S(2)}) copy-start(f32[64,2560]{1,0:T(8,128)} %copy-done.5) | copy-start | bytes 1966084
  992.9 276.1 %copy-start.27 = (f32[64]{0:T(128)S(1)}, f32[64]{0:T(128)}, u32[]{:S(2)}) copy-start(f32[64]{0:T(128)} %get-tuple-element.231) | copy-start | bytes 772
  998.7 16.2 %collective-permute-start.4 = (f32[64,128]{1,0:T(8,128)S(1)}, f32[64,128]{1,0:T(8,128)S(1)}, u32[]{:S(2)}, u32[]{:S(2)}) collective-permute-start(f32[64,128]{1,0:T(8,128)S(1)} %get-tuple-element.214), channel_id=1, source_target_pairs={{32,0},{64,32},{96,64},{128,96},{160,128},{192,160},{224,192},{33,... | collective-permute-start | bytes 98312 | tf_op jit(solution)/shard_map/ppermute | solution.py:14
  1000.6 14.3 %collective-permute-start.7 = (f32[64,128]{1,0:T(8,128)S(1)}, f32[64,128]{1,0:T(8,128)S(1)}, u32[]{:S(2)}, u32[]{:S(2)}) collective-permute-start(f32[64,128]{1,0:T(8,128)S(1)} %get-tuple-element.215), channel_id=1, source_target_pairs={{0,1},{1,2},{2,3},{3,4},{4,5},{5,6},{6,7},{7,8},{8,9},{9,10},{10,1... | collective-permute-start | bytes 98312 | tf_op jit(solution)/shard_map/ppermute | solution.py:14
  1002.5 12.3 collective-permute-start.6
  1003.8 11.1 collective-permute-start.5
Sparse Core Ops, SparseCore 0:
  108.4 256.2 all-reduce.10
  608.6 250.7 all-reduce.12
  1009.7 256.5 all-reduce.14
where the time goes:
time: 1300 us; the launch traced here: 1280 us
  waiting for transfers between devices  750 us (58%)
  other arithmetic  308 us (24%)
  matrix products  101 us (8%)
  local copies, waits for them, and re-layouts  93.4 us (7%)
  starting transfers between devices  17.9 us (1%)
  between operations  15 us (1%)
    psum x2, waiting for transfers between devices, coarse_total(): return lax.psum(table, ('gx', 'gy'))  503 us
    psum x1, waiting for transfers between devices, local(): lax.psum((grad_edge_in, grad_edge_out, grad_node_in, grad_node_out, grad_...  246 us
    scatter-add x1, other arithmetic, coarse_edge(): gathered = nodes[:, coarse_edges[0]]  104 us
    scatter-add x1, other arithmetic, coarse_edge(): summed = jnp.zeros_like(nodes).at[:, coarse_edges[1]].add(gathered)  90.5 us
    scatter-add x1, other arithmetic, fine_update(): sender_part[:, sources]  88 us
    dot_general x40, matrix products, matmul(): jnp.dot(left_side, right_side, precision=lax.Precision.HIGHEST, preferred...  80.9 us
    gather x1, local copies, waits for them, and re-layouts, fine_update(): sender_part[:, sources]  54.7 us
  transfers between devices with their start and end apart: 11, of which 3 were waited for; matrix products, arithmetic and copies ran while one was open for 2% of the time, Pallas kernels for 0%

commit v1 on v0

--- a/solution.py
+++ b/solution.py
@@ -205,17 +205,20 @@
     )
     fine_biases = jnp.stack([grad_edge_bias, grad_node_bias, grad_up_bias])
     summed = lax.psum(
-        (
-            grad_edge_in,
-            grad_edge_out,
-            grad_node_in,
-            grad_node_out,
-            grad_mix,
-            grad_up_in,
-            grad_up_out,
-            fine_biases,
+        lax.psum(
+            (
+                grad_edge_in,
+                grad_edge_out,
+                grad_node_in,
+                grad_node_out,
+                grad_mix,
+                grad_up_in,
+                grad_up_out,
+                fine_biases,
+            ),
+            "gx",
         ),
-        ("gx", "gy"),
+        "gy",
     )
     grad_biases = jnp.stack([summed[7][0], summed[7][1], grad_coarse_bias, summed[7][2]])
     return (

time: 1300 us -> 1260 us (0.969)
  waiting for transfers between devices: 750 us -> 710 us
    psum x1, waiting for transfers between devices: 246 us -> 61.1 us  [local(): lax.psum((grad_edge_in, grad_edge_out, grad_node_in, grad_node_out, grad_...]
    psum x0 -> x1, waiting for transfers between devices: none -> 146 us  [local(): lax.psum(lax.psum((grad_edge_in, grad_edge_out, grad_node_in, grad_node_o...]
  transfers between devices with their start and end apart: 11 -> 12, of which waited for: 3 -> 4; matrix products, arithmetic and copies ran while one was open for 2% -> 2% of each run, Pallas kernels for 0% -> 0%
where the time goes in v1:
time: 1260 us; the launch traced here: 1240 us
  waiting for transfers between devices  710 us (56%)
  other arithmetic  308 us (24%)
  matrix products  99.8 us (8%)
  local copies, waits for them, and re-layouts  93.4 us (7%)
  starting transfers between devices  17.9 us (1%)
  between operations  15 us (1%)
    psum x2, waiting for transfers between devices, coarse_total(): return lax.psum(table, ('gx', 'gy'))  503 us
    psum x1, waiting for transfers between devices, local(): lax.psum(lax.psum((grad_edge_in, grad_edge_out, grad_node_in, grad_node_o...  146 us
    scatter-add x1, other arithmetic, coarse_edge(): gathered = nodes[:, coarse_edges[0]]  104 us
    scatter-add x1, other arithmetic, coarse_edge(): summed = jnp.zeros_like(nodes).at[:, coarse_edges[1]].add(gathered)  90.4 us
    scatter-add x1, other arithmetic, fine_update(): sender_part[:, sources]  88 us
    dot_general x40, matrix products, matmul(): jnp.dot(left_side, right_side, precision=lax.Precision.HIGHEST, preferred...  80 us
    psum x1, waiting for transfers between devices, local(): lax.psum((grad_edge_in, grad_edge_out, grad_node_in, grad_node_out, grad_...  61.1 us
    gather x1, local copies, waits for them, and re-layouts, fine_update(): sender_part[:, sources]  54.8 us
  transfers between devices with their start and end apart: 12, of which 4 were waited for; matrix products, arithmetic and copies ran while one was open for 2% of the time, Pallas kernels for 0%

profile of v1, /device:TPU:4, one launch (start us, length us, event | category | flops | bytes accessed | tf_op | source)
XLA Modules:
  0.0 1244.0 jit_solution(6480068582541981289)
XLA Ops:
  11.8 4.5 collective-permute-start.2
  16.3 1.9 collective-permute-start.1
  18.3 2.4 collective-permute-start
  24.3 2.9 fusion.81
  27.2 2.9 fusion.102
  35.8 54.8 %gather_fusion.1 = f32[16384,64]{1,0:T(8,128)} fusion(f32[64,2560]{0,1:T(8,128)S(1)} %copy.65, s32[16384]{0:T(1024)S(1)} %broadcast_clamp_fusion), kind=kCustom, calls=%fused_computation.1 | custom fusion | bytes 8454144 | tf_op jit(solution)/shard_map/jvp()/gather | solution.py:33
  90.6 4.8 multiply_reduce_fusion
  100.5 7.0 while.44
  100.5 3.5 fusion.178
  104.0 3.5 fusion.178
  110.1 254.5 %all-reduce.13.cloned.1.call-done = f32[64,2048]{1,0:T(8,128)} async-done(((f32[64,2048]{1,0:T(8,128)}), f32[64,2048]{1,0:T(8,128)}) %all-reduce.13.cloned.1.call-update) | async-done | bytes 524304 | tf_op jit(solution)/shard_map/psum | solution.py:119
  370.3 90.4 %scatter_custom_fusion = f32[64,2048]{0,1:T(8,128)S(1)} fusion(s32[8192]{0:T(1024)} %bitcast.245, f32[64,2048]{0,1:T(8,128)} %copy.67, s32[8192]{0:T(1024)} %broadcast_clamp_fusion.2, f32[]{:T(128)} %constant.19.clone.1), kind=kCustom, calls=%fused_computation.44 | custom fusion | flops 524288 | bytes 524800 | tf_op jit(solution)/shard_map/jvp()/scatter-add | solution.py:49
  460.7 2.1 fusion.29
  462.9 11.0 while.42
  462.9 5.5 fusion.174
  468.4 5.5 fusion.174
  473.9 2.2 fusion.96
  476.1 2.3 convolution_bitcast_fusion.14
  478.4 2.6 fusion.37
  484.9 10.3 while.45
  484.9 5.1 fusion.180
  490.0 5.2 fusion.180
  495.2 2.5 convolution_bitcast_fusion.7
  497.7 2.4 copy.71
  500.1 2.4 copy.70
  502.4 103.6 %scatter_custom_fusion.1 = f32[64,2048]{0,1:T(8,128)} fusion(f32[64,2048]{0,1:T(8,128)} %copy.71, s32[8192]{0:T(1024)} %bitcast.243, f32[]{:T(128)} %constant.19.clone.1, pred[8192]{0:T(1024)(128)(4,1)S(1)} %compare_and_fusion, f32[64,2048]{0,1:T(8,128)} %copy.70, s32[8192]{0:T(1024)S(1)} %broadcast_clamp_fusion.1), kind=kCustom, calls=%fused_computation.42 | custom fusion | flops 1048576 | bytes 1614336 | tf_op jit(solution)/shard_map/transpose(jvp())/scatter-add | solution.py:48
  606.0 2.3 copy.72
  608.4 2.4 fusion.55
  610.8 248.3 %all-reduce.15.cloned.1.call-done = f32[64,2048]{1,0:T(8,128)} async-done(((f32[64,2048]{1,0:T(8,128)}), f32[64,2048]{1,0:T(8,128)}) %all-reduce.15.cloned.1.call-update) | async-done | bytes 524304 | tf_op jit(solution)/shard_map/psum | solution.py:119
  859.2 2.6 fusion.100
  864.3 8.9 while.43
  864.3 4.4 fusion.176
  868.8 4.4 fusion.176
  877.0 2.6 fusion.62
  888.7 5.7 fusion.21
  894.4 3.3 copy-done.1
  897.7 2.5 fusion.95
  900.1 2.5 fusion.104
  903.9 88.0 %scatter_custom_fusion.2 = f32[64,2560]{0,1:T(8,128)S(1)} fusion(s32[16384]{0:T(1024)S(1)} %bitcast.240, f32[16384,64]{1,0:T(8,128)} %bitcast.227, f32[]{:T(128)} %constant.19.clone.1), kind=kCustom, calls=%fused_computation.85 | custom fusion | flops 1048576 | bytes 655872 | tf_op jit(solution)/shard_map/transpose(jvp())/scatter-add | solution.py:33
  991.9 2.2 fusion.103
  997.4 1.9 collective-permute-start.4
  999.4 1.9 collective-permute-start.7
  1002.6 1.9 collective-permute-start.5
  1008.4 2.5 fusion.65
  1011.0 61.1 %all-reduce.19.cloned.1.call-done = (f32[64,128]{1,0:T(8,128)}, f32[64,64]{1,0:T(8,128)}, f32[64,128]{1,0:T(8,128)}, f32[64,64]{1,0:T(8,128)}, f32[64,64]{1,0:T(...) async-done(((f32[64,128]{1,0:T(8,128)}, f32[64,64]{1,0:T(8,128)}, f32[64,128]{1,0:T(8,128)}, f32[64,64]{1,0:T(8,128)}, f32[64,64]{1,0:T(8,128)}, ...) | async-done | bytes 164624 | tf_op jit(solution)/shard_map/psum | solution.py:208
  1072.1 2.4 fusion.108
  1075.0 3.7 scatter_fusion
  1079.8 145.7 %all-reduce.17.cloned.1.call-done = (f32[64,128]{1,0:T(8,128)}, f32[64,64]{1,0:T(8,128)}, f32[64,128]{1,0:T(8,128)}, f32[64,64]{1,0:T(8,128)}, f32[64,64]{1,0:T(...) async-done(((f32[64,128]{1,0:T(8,128)}, f32[64,64]{1,0:T(8,128)}, f32[64,128]{1,0:T(8,128)}, f32[64,64]{1,0:T(8,128)}, f32[64,64]{1,0:T(8,128)}, ...) | async-done | bytes 164624 | tf_op jit(solution)/shard_map/psum | solution.py:207
  (162 shorter events, 69.3 us)
Async XLA Ops:
  7.2 359.9 %copy-start = (f32[64,64]{1,0:T(8,128)S(1)}, f32[64,64]{1,0:T(8,128)}, u32[]{:S(2)}) copy-start(f32[64,64]{1,0:T(8,128)} %param.37) | copy-start | bytes 49156
  7.2 357.4 %all-reduce.13.cloned.1.call-start = ((), (), s32[]{:S(2)}) async-start(), calls=%async_computation | async-start | bytes 1048576 | tf_op jit(solution)/shard_map/psum | solution.py:119
  10.5 22.6 %collective-permute-start.3 = (f32[64,128]{1,0:T(8,128)S(1)}, f32[64,128]{1,0:T(8,128)S(1)}, u32[]{:S(2)}, u32[]{:S(2)}) collective-permute-start(f32[64,128]{1,0:T(8,128)S(1)} %get-tuple-element.226), channel_id=1, source_target_pairs={{1,0},{2,1},{3,2},{4,3},{5,4},{6,5},{7,6},{8,7},{9,8},{10,9},{11,1... | collective-permute-start | bytes 98312 | tf_op jit(solution)/shard_map/ppermute | solution.py:14
  11.8 21.3 %collective-permute-start.2 = (f32[64,128]{1,0:T(8,128)S(1)}, f32[64,128]{1,0:T(8,128)S(1)}, u32[]{:S(2)}, u32[]{:S(2)}) collective-permute-start(f32[64,128]{1,0:T(8,128)S(1)} %get-tuple-element.227), channel_id=1, source_target_pairs={{0,1},{1,2},{2,3},{3,4},{4,5},{5,6},{6,7},{7,8},{8,9},{9,10},{10,1... | collective-permute-start | bytes 98312 | tf_op jit(solution)/shard_map/ppermute | solution.py:14
  16.3 16.7 %collective-permute-start.1 = (f32[64,128]{1,0:T(8,128)S(1)}, f32[64,128]{1,0:T(8,128)S(1)}, u32[]{:S(2)}, u32[]{:S(2)}) collective-permute-start(f32[64,128]{1,0:T(8,128)S(1)} %get-tuple-element.228), channel_id=1, source_target_pairs={{32,0},{64,32},{96,64},{128,96},{160,128},{192,160},{224,192},{33,... | collective-permute-start | bytes 98312 | tf_op jit(solution)/shard_map/ppermute | solution.py:14
  18.3 14.7 %collective-permute-start = (f32[64,128]{1,0:T(8,128)S(1)}, f32[64,128]{1,0:T(8,128)S(1)}, u32[]{:S(2)}, u32[]{:S(2)}) collective-permute-start(f32[64,128]{1,0:T(8,128)S(1)} %get-tuple-element.229), channel_id=1, source_target_pairs={{0,32},{32,64},{64,96},{96,128},{128,160},{160,192},{192,224},{1,3... | collective-permute-start | bytes 98312 | tf_op jit(solution)/shard_map/ppermute | solution.py:14
  23.7 6.4 copy-start.24
  23.7 12.1 copy-start.23
  27.2 63.4 %copy-start.3 = (f32[64,2048]{0,1:T(8,128)}, f32[64,2048]{0,1:T(8,128)S(1)}, u32[]{:S(2)}) copy-start(f32[64,2048]{0,1:T(8,128)S(1)} %fusion.81) | copy-start | bytes 1572868
  33.1 0.8 copy-start.5
  90.6 4.9 copy-start.22
  90.6 7.0 copy-start.18
  90.6 7.6 copy-start.2
  90.6 9.0 copy-start.29
  90.6 9.8 copy-start.16
  96.8 0.8 copy-start.7
  98.8 0.8 copy-start.15
  100.3 8.3 copy-start.9
  100.4 8.2 copy-start.26
  100.4 8.3 copy-start.19
  100.4 264.2 %copy-start.21 = (f32[64,64]{1,0:T(8,128)S(1)}, f32[64,64]{1,0:T(8,128)}, u32[]{:S(2)}) copy-start(f32[64,64]{1,0:T(8,128)} %param.36) | copy-start | bytes 49156
  107.4 353.2 %copy-start.20 = (f32[64,64]{1,0:T(8,128)S(1)}, f32[64,64]{1,0:T(8,128)}, u32[]{:S(2)}) copy-start(f32[64,64]{1,0:T(8,128)} %param.38) | copy-start | bytes 49156
  108.3 750.8 %all-reduce.15.cloned.1.call-start = ((), (), s32[]{:S(2)}) async-start(), calls=%async_computation.1 | async-start | bytes 1048576 | tf_op jit(solution)/shard_map/psum | solution.py:119
  366.3 0.8 copy-start.17
  462.8 11.1 copy-start.28
  462.8 15.5 %copy-start.25 = (f32[64,64]{1,0:T(8,128)S(1)}, f32[64,64]{1,0:T(8,128)}, u32[]{:S(2)}) copy-start(f32[64,64]{1,0:T(8,128)} %param.40) | copy-start | bytes 49156
  473.9 8.3 copy-start.10
  608.4 463.6 %all-reduce.19.cloned.1.call-start = ((), (), s32[]{:S(2)}) async-start(), calls=%async_computation.3 | async-start | bytes 462848 | tf_op jit(solution)/shard_map/psum | solution.py:208
  861.8 0.8 copy-start.11
  864.3 15.3 %copy-start.30 = (f32[64,64]{1,0:T(8,128)S(1)}, f32[64,64]{1,0:T(8,128)}, u32[]{:S(2)}) copy-start(f32[64,64]{1,0:T(8,128)} %param.35) | copy-start | bytes 49156
  873.2 0.8 copy-start.12
  874.0 7.4 copy-start.8
  874.0 14.6 %copy-start.4 = (f32[64,2048]{0,1:T(8,128)S(1)}, f32[64,2048]{0,1:T(8,128)}, u32[]{:S(2)}) copy-start(f32[64,2048]{0,1:T(8,128)} %copy-done.3) | copy-start | bytes 1572868
  877.0 5.7 copy-start.13
  894.4 3.3 copy-start.1
  897.7 4.9 copy-start.14
  897.7 94.2 %copy-start.6 = (f32[64,2560]{1,0:T(8,128)S(1)}, f32[64,2560]{1,0:T(8,128)}, u32[]{:S(2)}) copy-start(f32[64,2560]{1,0:T(8,128)} %copy-done.5) | copy-start | bytes 1966084
  991.9 236.3 %copy-start.27 = (f32[64]{0:T(128)S(1)}, f32[64]{0:T(128)}, u32[]{:S(2)}) copy-start(f32[64]{0:T(128)} %get-tuple-element.239) | copy-start | bytes 772
  997.4 77.3 %collective-permute-start.4 = (f32[64,128]{1,0:T(8,128)S(1)}, f32[64,128]{1,0:T(8,128)S(1)}, u32[]{:S(2)}, u32[]{:S(2)}) collective-permute-start(f32[64,128]{1,0:T(8,128)S(1)} %get-tuple-element.222), channel_id=1, source_target_pairs={{32,0},{64,32},{96,64},{128,96},{160,128},{192,160},{224,192},{33,... | collective-permute-start | bytes 98312 | tf_op jit(solution)/shard_map/ppermute | solution.py:14
  999.4 75.4 %collective-permute-start.7 = (f32[64,128]{1,0:T(8,128)S(1)}, f32[64,128]{1,0:T(8,128)S(1)}, u32[]{:S(2)}, u32[]{:S(2)}) collective-permute-start(f32[64,128]{1,0:T(8,128)S(1)} %get-tuple-element.223), channel_id=1, source_target_pairs={{0,1},{1,2},{2,3},{3,4},{4,5},{5,6},{6,7},{7,8},{8,9},{9,10},{10,1... | collective-permute-start | bytes 98312 | tf_op jit(solution)/shard_map/ppermute | solution.py:14
  1001.3 73.5 %collective-permute-start.6 = (f32[64,128]{1,0:T(8,128)S(1)}, f32[64,128]{1,0:T(8,128)S(1)}, u32[]{:S(2)}, u32[]{:S(2)}) collective-permute-start(f32[64,128]{1,0:T(8,128)S(1)} %get-tuple-element.224), channel_id=1, source_target_pairs={{1,0},{2,1},{3,2},{4,3},{5,4},{6,5},{7,6},{8,7},{9,8},{10,9},{11,1... | collective-permute-start | bytes 98312 | tf_op jit(solution)/shard_map/ppermute | solution.py:14
  1002.6 72.2 %collective-permute-start.5 = (f32[64,128]{1,0:T(8,128)S(1)}, f32[64,128]{1,0:T(8,128)S(1)}, u32[]{:S(2)}, u32[]{:S(2)}) collective-permute-start(f32[64,128]{1,0:T(8,128)S(1)} %get-tuple-element.225), channel_id=1, source_target_pairs={{0,32},{32,64},{64,96},{96,128},{128,160},{160,192},{192,224},{1,3... | collective-permute-start | bytes 98312 | tf_op jit(solution)/shard_map/ppermute | solution.py:14
  1008.1 217.4 %all-reduce.17.cloned.1.call-start = ((), (), s32[]{:S(2)}) async-start(), calls=%async_computation.2 | async-start | bytes 462848 | tf_op jit(solution)/shard_map/psum | solution.py:207
Sparse Core Ops, SparseCore 0:
  108.4 256.1 all-reduce.12
  608.5 250.5 all-reduce.14
  1008.2 63.7 all-reduce.18
  1076.9 148.5 all-reduce.16
